TPU v7x, 512 devices: a whole 4x8x8 slice. The times are simulated.
512 devices in a mesh: wide: 64 (over y, z_hi, core), batch: 8 (over z_lo, x).
Axes of the slice: x: 4, y: 8, z: 8 (z_hi: 4, z_lo: 2; z = z_hi * 2 + z_lo), core: 2. Of those that a mesh axis runs over, the one named last changes fastest.
Arguments:
- integrals: bfloat16 [1536, 64, 640], P('wide'), may hold values from -0.8984375 to 0.8984375
- vir_coeff: bfloat16 [640, 512], P(None, 'batch'), may hold values from -0.25 to 0.25
- occ_energy: float32 [64], replicated, may hold values from -1.6 to -0.4
- vir_energy: float32 [512], replicated, may hold values from 0.2 to 3
- kappas: float32 [8], replicated, may hold values from 0.1 to 3
Outputs:
- density: bfloat16 [8, 64, 512, 1536], P(None, 'wide', 'batch')
All inputs are finite; a program needn't handle non-finite values.
Results may differ from a plain program's by a relative error of at most 0.0051.
Values may be sent and summed in bfloat16 or wider, within the bound.
A program may use at most 64 MiB of HBM per device.

v0:
```python
import jax
import jax.numpy as jnp
from jax import lax
from jax.sharding import PartitionSpec as P

HALF = 2


def from_behind(shard, axis, by):
    peers = lax.axis_size(axis)
    return lax.ppermute(shard, axis, [(i, (i + by) % peers) for i in range(peers)])


def pair_density(own_slice, partner, own_energy, partner_energy, row_energy, vir_energy, kappas):
    coulomb = lax.dot_general(
        own_slice, partner, (((0,), (0,)), ((), ())), preferred_element_type=jnp.float32
    )
    denominator = row_energy[:, None] + vir_energy[None, :] - own_energy - partner_energy
    damping = 1.0 - jnp.exp(-kappas[:, None, None] * denominator[None])
    amplitude = (-coulomb[None] * (damping * damping) / denominator[None]).astype(jnp.bfloat16)
    flat = amplitude.reshape(-1, amplitude.shape[2])
    density = lax.dot_general(
        flat, partner, (((1,), (1,)), ((), ())), preferred_element_type=jnp.float32
    )
    return density.reshape(kappas.shape[0], own_slice.shape[1], partner.shape[0])


def on_device(integrals, vir_coeff, occ_energy, vir_energy, kappas):
    aux_local, occ_count, basis = integrals.shape
    vir_local = vir_coeff.shape[1]
    batch_index = lax.axis_index("batch")
    wide_index = lax.axis_index("wide")
    flat_ints = integrals.reshape(aux_local * occ_count, basis)
    row_energy = lax.dynamic_slice_in_dim(vir_energy, batch_index * vir_local, vir_local, 0)
    own_energy = lax.dynamic_slice_in_dim(occ_energy, wide_index, 1, 0)[0]

    def term(partner, offset, own_slice):
        partner_index = (wide_index + offset) % occ_count
        partner_energy = lax.dynamic_slice_in_dim(occ_energy, partner_index, 1, 0)[0]
        return pair_density(
            own_slice, partner, own_energy, partner_energy, row_energy, vir_energy, kappas
        )

    transformed = jnp.dot(flat_ints, vir_coeff, preferred_element_type=jnp.float32).astype(
        jnp.bfloat16
    )
    transformed = transformed.reshape(aux_local, occ_count, vir_local)
    own_slice = lax.all_to_all(transformed, "wide", split_axis=1, concat_axis=0, tiled=True)[
        :, 0, :
    ]
    own_full = lax.all_gather(own_slice, "batch", axis=1, tiled=True)
    partner = from_behind(own_full, "wide", HALF)
    density = term(partner, -HALF, own_slice)
    for offset in range(1 - HALF, HALF + 1):
        partner = from_behind(partner, "wide", -1)
        density = density + term(partner, offset, own_slice)
    return density.astype(jnp.bfloat16)[:, None, :, :]


def solution(mesh):
    return jax.shard_map(
        on_device,
        mesh=mesh,
        in_specs=(P("wide", None, None), P(None, "batch"), P(), P(), P()),
        out_specs=P(None, "wide", "batch", None),
        check_vma=False,
    )
```

profile of v0, /device:TPU:31, one launch (start us, length us, event | category | flops | bytes accessed | tf_op | source)
XLA Modules:
  0.0 345.7 jit_solution(11318890819423333155)
XLA Ops:
  6.5 0.0 copy-start
  6.5 0.0 all-gather.2.cloned.1.call-start
  6.5 1.5 copy-done
  8.1 1.6 convolution_convert_fusion
  9.7 0.2 reshape.201
  9.9 0.4 copy.16
  10.3 0.2 reshape.207
  10.6 28.0 %all_to_all.15 = bf16[64,2,768]{2,1,0:T(2,128)(2,1)S(1)} all-to-all(bf16[64,2,768]{2,1,0:T(2,128)(2,1)S(1)} %reshape.207), channel_id=1, replica_groups=mesh['wide'=64,'batch'=8] {'wide'}, dimensions={0} | all-to-all | bytes 393216 | tf_op jit(solution)/shard_map/all_to_all | solution.py:48
  38.6 0.3 reshape.208
  38.9 0.8 copy.17
  39.7 0.0 all-gather.2.cloned.1.call-update
  39.7 0.0 copy-start.7
  39.8 0.0 copy-start.6
  39.8 0.0 copy-start.5
  39.8 34.2 %all-gather.2.cloned.1.call-done = bf16[1536,512]{0,1:T(8,128)(2,1)} async-done(((bf16[1536,64]{0,1:T(8,128)(2,1)}), bf16[1536,512]{0,1:T(8,128)(2,1)}) %all-gather.2.cloned.1.call-update) | async-done | bytes 1572880 | tf_op jit(solution)/shard_map/all_gather | solution.py:51
  73.9 2.6 copy.18
  76.5 4.3 %collective-permute-start = (bf16[1536,512]{1,0:T(8,128)(2,1)}, bf16[1536,512]{1,0:T(8,128)(2,1)S(1)}, u32[]{:S(2)}, u32[]{:S(2)}) collective-permute-start(bf16[1536,512]{1,0:T(8,128)(2,1)} %copy.18), channel_id=1, source_target_pairs={{0,16},{8,24},{16,32},{24,40},{32,48},{40,56},{48,64},{56,72},{64,... | collective-permute-start | bytes 4718600 | tf_op jit(solution)/shard_map/ppermute | solution.py:11
  80.9 56.8 %collective-permute-done = bf16[1536,512]{1,0:T(8,128)(2,1)S(1)} collective-permute-done((bf16[1536,512]{1,0:T(8,128)(2,1)}, bf16[1536,512]{1,0:T(8,128)(2,1)S(1)}, u32[]{:S(2)}, u32[]{:S(2)}) %collective-permute-start) | collective-permute-done | bytes 1572896 | tf_op jit(solution)/shard_map/ppermute | solution.py:11
  137.7 9.7 %collective-permute-start.1 = (bf16[1536,512]{1,0:T(8,128)(2,1)S(1)}, bf16[1536,512]{1,0:T(8,128)(2,1)S(1)}, u32[]{:S(2)}, u32[]{:S(2)}) collective-permute-start(bf16[1536,512]{1,0:T(8,128)(2,1)S(1)} %collective-permute-done), channel_id=1, source_target_pairs={{0,504},{8,0},{16,8},{24,16},{32,24},{40,32},{48,40},{56,48},{64,5... | collective-permute-start | bytes 4718600 | tf_op jit(solution)/shard_map/ppermute | solution.py:11
  147.4 61.3 %collective-permute-done.1 = bf16[1536,512]{1,0:T(8,128)(2,1)S(1)} collective-permute-done((bf16[1536,512]{1,0:T(8,128)(2,1)S(1)}, bf16[1536,512]{1,0:T(8,128)(2,1)S(1)}, u32[]{:S(2)}, u32[]{:S(2)}) %collective-permute-start.1) | collective-permute-done | bytes 1572896 | tf_op jit(solution)/shard_map/ppermute | solution.py:11
  208.8 1.2 copy-done.1
  210.0 1.9 collective-permute-start.2
  211.9 51.3 %collective-permute-done.2 = bf16[1536,512]{1,0:T(8,128)(2,1)} collective-permute-done((bf16[1536,512]{1,0:T(8,128)(2,1)S(1)}, bf16[1536,512]{1,0:T(8,128)(2,1)}, u32[]{:S(2)}, u32[]{:S(2)}) %collective-permute-start.2) | collective-permute-done | bytes 1572896 | tf_op jit(solution)/shard_map/ppermute | solution.py:11
  263.2 0.0 copy-done.3
  263.2 1.9 collective-permute-start.3
  265.2 0.0 copy-done.7
  265.2 0.0 copy-done.6
  265.2 0.0 copy-start.4
  265.3 0.1 dynamic_slice.21
  265.3 0.0 copy-done.5
  265.3 0.7 fusion.38
  266.0 3.7 %fusion.28 = (f32[64,512]{1,0:T(8,128)S(1)}, f32[64,512]{1,0:T(8,128)S(1)}, f32[64,512]{1,0:T(8,128)S(1)}, f32[64,512]{1,0:T(8,128)S(1)}, f32[64,512]{1,0:T(8,128)S(1)}) fusion(f32[]{:T(128)} %bitcast.15, f32[]{:T(128)} %bitcast.6, f32[512]{0:T(512)S(1)} %copy-done.6, f32[64]{0:T(128)S(1)} %dynamic_slice.21, f32[]{:T(128)} %bitcast.13, f32[]{:T(128)} %bitcast.11, ...), kind=kLoop, calls=%fused_computation.44 | loop fusion | flops 229376 | bytes 657688 | tf_op jit(solution)/shard_map/sub | solution.py:18
  269.8 1.8 convolution_negate_fusion.4
  271.6 0.0 copy-done.4
  271.6 0.0 copy-start.2
  271.6 1.1 fusion.6
  272.7 0.3 copy-done.2
  273.0 0.4 convolution_negate_fusion.3
  273.4 38.6 %collective-permute-done.3 = bf16[1536,512]{1,0:T(8,128)(2,1)} collective-permute-done((bf16[1536,512]{1,0:T(8,128)(2,1)}, bf16[1536,512]{1,0:T(8,128)(2,1)}, u32[]{:S(2)}, u32[]{:S(2)}) %collective-permute-start.3) | collective-permute-done | bytes 1572896 | tf_op jit(solution)/shard_map/ppermute | solution.py:11
  312.0 1.9 collective-permute-start.4
  313.9 1.1 convolution_add_fusion.3
  315.0 1.8 convolution_negate_fusion.2
  316.8 2.5 convolution_add_fusion.2
  319.3 1.8 convolution_negate_fusion.1
  321.1 2.5 convolution_add_fusion.1
  323.6 12.6 %collective-permute-done.4 = bf16[1536,512]{1,0:T(8,128)(2,1)S(1)} collective-permute-done((bf16[1536,512]{1,0:T(8,128)(2,1)}, bf16[1536,512]{1,0:T(8,128)(2,1)S(1)}, u32[]{:S(2)}, u32[]{:S(2)}) %collective-permute-start.4) | collective-permute-done | bytes 1572896 | tf_op jit(solution)/shard_map/ppermute | solution.py:11
  336.2 0.4 convolution_negate_fusion
  336.6 2.2 fusion.1
  (3 shorter events, 0.0 us)
Async XLA Ops:
  6.5 1.5 copy-start
  6.5 67.4 %all-gather.2.cloned.1.call-start = ((), (), s32[]{:S(2)}) async-start(), calls=%async_computation.1 | async-start | bytes 1769472 | tf_op jit(solution)/shard_map/all_gather | solution.py:51
  39.7 225.4 %copy-start.7 = (f32[8]{0:T(128)S(1)}, f32[8]{0:T(128)}, u32[]{:S(2)}) copy-start(f32[8]{0:T(128)} %param.9) | copy-start | bytes 100
  39.8 225.5 %copy-start.6 = (f32[512]{0:T(512)S(1)}, f32[512]{0:T(512)}, u32[]{:S(2)}) copy-start(f32[512]{0:T(512)} %param.8) | copy-start | bytes 6148
  39.8 225.6 %copy-start.5 = (f32[64]{0:T(128)S(1)}, f32[64]{0:T(128)}, u32[]{:S(2)}) copy-start(f32[64]{0:T(128)} %param.7) | copy-start | bytes 772
  76.5 61.2 %collective-permute-start = (bf16[1536,512]{1,0:T(8,128)(2,1)}, bf16[1536,512]{1,0:T(8,128)(2,1)S(1)}, u32[]{:S(2)}, u32[]{:S(2)}) collective-permute-start(bf16[1536,512]{1,0:T(8,128)(2,1)} %copy.18), channel_id=1, source_target_pairs={{0,16},{8,24},{16,32},{24,40},{32,48},{40,56},{48,64},{56,72},{64,... | collective-permute-start | bytes 4718600 | tf_op jit(solution)/shard_map/ppermute | solution.py:11
  137.7 125.5 %copy-start.3 = (bf16[1536,512]{1,0:T(8,128)(2,1)}, bf16[1536,512]{1,0:T(8,128)(2,1)S(1)}, u32[]{:S(2)}) copy-start(bf16[1536,512]{1,0:T(8,128)(2,1)S(1)} %collective-permute-done) | copy-start | bytes 4718596
  137.7 71.1 %collective-permute-start.1 = (bf16[1536,512]{1,0:T(8,128)(2,1)S(1)}, bf16[1536,512]{1,0:T(8,128)(2,1)S(1)}, u32[]{:S(2)}, u32[]{:S(2)}) collective-permute-start(bf16[1536,512]{1,0:T(8,128)(2,1)S(1)} %collective-permute-done), channel_id=1, source_target_pairs={{0,504},{8,0},{16,8},{24,16},{32,24},{40,32},{48,40},{56,48},{64,5... | collective-permute-start | bytes 4718600 | tf_op jit(solution)/shard_map/ppermute | solution.py:11
  208.8 1.2 copy-start.1
  210.0 53.2 %collective-permute-start.2 = (bf16[1536,512]{1,0:T(8,128)(2,1)S(1)}, bf16[1536,512]{1,0:T(8,128)(2,1)}, u32[]{:S(2)}, u32[]{:S(2)}) collective-permute-start(bf16[1536,512]{1,0:T(8,128)(2,1)S(1)} %collective-permute-done.1), channel_id=1, source_target_pairs={{0,504},{8,0},{16,8},{24,16},{32,24},{40,32},{48,40},{56,48},{64,5... | collective-permute-start | bytes 4718600 | tf_op jit(solution)/shard_map/ppermute | solution.py:11
  263.2 48.8 %collective-permute-start.3 = (bf16[1536,512]{1,0:T(8,128)(2,1)}, bf16[1536,512]{1,0:T(8,128)(2,1)}, u32[]{:S(2)}, u32[]{:S(2)}) collective-permute-start(bf16[1536,512]{1,0:T(8,128)(2,1)} %collective-permute-done.2), channel_id=1, source_target_pairs={{0,504},{8,0},{16,8},{24,16},{32,24},{40,32},{48,40},{56,48},{64,5... | collective-permute-start | bytes 4718600 | tf_op jit(solution)/shard_map/ppermute | solution.py:11
  265.2 6.3 %copy-start.4 = (bf16[1536,512]{1,0:T(8,128)(2,1)S(1)}, bf16[1536,512]{1,0:T(8,128)(2,1)}, u32[]{:S(2)}) copy-start(bf16[1536,512]{1,0:T(8,128)(2,1)} %copy-done.3) | copy-start | bytes 4718596
  271.6 1.4 copy-start.2
  312.0 24.2 %collective-permute-start.4 = (bf16[1536,512]{1,0:T(8,128)(2,1)}, bf16[1536,512]{1,0:T(8,128)(2,1)S(1)}, u32[]{:S(2)}, u32[]{:S(2)}) collective-permute-start(bf16[1536,512]{1,0:T(8,128)(2,1)} %collective-permute-done.3), channel_id=1, source_target_pairs={{0,504},{8,0},{16,8},{24,16},{32,24},{40,32},{48,40},{56,48},{64,5... | collective-permute-start | bytes 4718600 | tf_op jit(solution)/shard_map/ppermute | solution.py:11
Sparse Core Ops, SparseCore 0:
  39.9 34.0 all-gather.1
where the time goes:
time: 346 us
  waiting for transfers between devices  255 us (74%)
  blocking collectives  28 us (8%)
  starting transfers between devices  19.8 us (6%)
  matrix products  17.2 us (5%)
  between operations  13.7 us (4%)
  local copies, waits for them, and re-layouts  8.39 us (2%)
  other arithmetic  3.73 us (1%)
    ppermute x5, waiting for transfers between devices, from_behind(): lax.ppermute(shard, axis, [(i, (i + by) % peers) for i in range(peers)])  221 us
    all_gather x1, waiting for transfers between devices, on_device(): own_full = lax.all_gather(own_slice, 'batch', axis=1, tiled=True)  34.2 us
    all_to_all x1, blocking collectives, on_device(): lax.all_to_all(transformed, 'wide', split_axis=1, concat_axis=0, tiled=True)  28 us
    ppermute x5, starting transfers between devices, from_behind(): lax.ppermute(shard, axis, [(i, (i + by) % peers) for i in range(peers)])  19.8 us
    dot_general x5, matrix products, pair_density(): lax.dot_general(flat, partner, (((1,), (1,)), ((), ())), preferred_elemen...  9.32 us
  transfers between devices with their start and end apart: 6, of which 6 were waited for; matrix products, arithmetic and copies ran while one was open for 5% of the time, Pallas kernels for 0%

commit v1 on v0

--- a/solution.py
+++ b/solution.py
@@ -48,7 +48,8 @@
     own_slice = lax.all_to_all(transformed, "wide", split_axis=1, concat_axis=0, tiled=True)[
         :, 0, :
     ]
-    own_full = lax.all_gather(own_slice, "batch", axis=1, tiled=True)
+    sent = jnp.stack([own_slice] * lax.axis_size("batch"))
+    own_full = jnp.concatenate(lax.all_to_all(sent, "batch", 0, 0), axis=1)
     partner = from_behind(own_full, "wide", HALF)
     density = term(partner, -HALF, own_slice)
     for offset in range(1 - HALF, HALF + 1):

time: 346 us -> 314 us (0.908)
  the two profiles are of different devices: /device:TPU:31 before, /device:TPU:57 now
where the time goes in v1:
time: 314 us
  waiting for transfers between devices  218 us (69%)
  blocking collectives  51.4 us (16%)
  matrix products  17.2 us (5%)
  starting transfers between devices  15.3 us (5%)
  local copies, waits for them, and re-layouts  7.87 us (3%)
  other arithmetic  3.79 us (1%)
    ppermute x5, waiting for transfers between devices, from_behind(): lax.ppermute(shard, axis, [(i, (i + by) % peers) for i in range(peers)])  218 us
    all_to_all x1, blocking collectives, on_device(): lax.all_to_all(transformed, 'wide', split_axis=1, concat_axis=0, tiled=True)  27.3 us
    all_to_all x1, blocking collectives, on_device(): own_full = jnp.concatenate(lax.all_to_all(sent, 'batch', 0, 0), axis=1)  24.1 us
    ppermute x5, starting transfers between devices, from_behind(): lax.ppermute(shard, axis, [(i, (i + by) % peers) for i in range(peers)])  15.3 us
    dot_general x5, matrix products, pair_density(): lax.dot_general(flat, partner, (((1,), (1,)), ((), ())), preferred_elemen...  9.31 us
  transfers between devices with their start and end apart: 5, of which 5 were waited for; matrix products, arithmetic and copies ran while one was open for 6% of the time, Pallas kernels for 0%

profile of v1, /device:TPU:57, one launch (start us, length us, event | category | flops | bytes accessed | tf_op | source)
XLA Modules:
  0.0 313.8 jit_solution(3556500056317765634)
XLA Ops:
  0.0 0.0 copy-start
  0.0 1.5 copy-done
  1.5 1.6 convolution_convert_fusion
  3.2 0.2 reshape.210
  3.4 0.4 copy.7
  3.8 0.2 reshape.218
  4.0 27.3 %all_to_all.20 = bf16[64,2,768]{2,1,0:T(2,128)(2,1)S(1)} all-to-all(bf16[64,2,768]{2,1,0:T(2,128)(2,1)S(1)} %reshape.218), channel_id=1, replica_groups=mesh['wide'=64,'batch'=8] {'wide'}, dimensions={0} | all-to-all | bytes 393216 | tf_op jit(solution)/shard_map/all_to_all | solution.py:48
  31.3 0.3 reshape.219
  31.6 0.2 copy.8
  31.8 0.1 stack.3
  31.9 24.1 %all_to_all.21 = bf16[8,1536,64]{1,2,0:T(8,128)(2,1)} all-to-all(bf16[8,1536,64]{1,2,0:T(8,128)(2,1)S(1)} %stack.3), channel_id=1, replica_groups=mesh['wide'=64,'batch'=8] {'batch'}, dimensions={0} | all-to-all | bytes 3145728 | tf_op jit(solution)/shard_map/all_to_all | solution.py:52
  56.0 0.0 copy-start.7
  56.0 0.0 copy-start.6
  56.0 0.0 copy-start.5
  56.0 2.6 copy.9
  58.6 1.9 collective-permute-start
  60.5 62.7 %collective-permute-done = bf16[1536,512]{1,0:T(8,128)(2,1)S(1)} collective-permute-done((bf16[1536,512]{1,0:T(8,128)(2,1)}, bf16[1536,512]{1,0:T(8,128)(2,1)S(1)}, u32[]{:S(2)}, u32[]{:S(2)}) %collective-permute-start) | collective-permute-done | bytes 1572896 | tf_op jit(solution)/shard_map/ppermute | solution.py:11
  123.2 0.0 copy-start.3
  123.2 7.7 %collective-permute-start.1 = (bf16[1536,512]{1,0:T(8,128)(2,1)S(1)}, bf16[1536,512]{1,0:T(8,128)(2,1)S(1)}, u32[]{:S(2)}, u32[]{:S(2)}) collective-permute-start(bf16[1536,512]{1,0:T(8,128)(2,1)S(1)} %collective-permute-done), channel_id=1, source_target_pairs={{0,504},{8,0},{16,8},{24,16},{32,24},{40,32},{48,40},{56,48},{64,5... | collective-permute-start | bytes 4718600 | tf_op jit(solution)/shard_map/ppermute | solution.py:11
  130.9 38.2 %collective-permute-done.1 = bf16[1536,512]{1,0:T(8,128)(2,1)S(1)} collective-permute-done((bf16[1536,512]{1,0:T(8,128)(2,1)S(1)}, bf16[1536,512]{1,0:T(8,128)(2,1)S(1)}, u32[]{:S(2)}, u32[]{:S(2)}) %collective-permute-start.1) | collective-permute-done | bytes 1572896 | tf_op jit(solution)/shard_map/ppermute | solution.py:11
  169.1 1.2 copy-done.1
  170.3 1.9 collective-permute-start.2
  172.2 61.3 %collective-permute-done.2 = bf16[1536,512]{1,0:T(8,128)(2,1)} collective-permute-done((bf16[1536,512]{1,0:T(8,128)(2,1)S(1)}, bf16[1536,512]{1,0:T(8,128)(2,1)}, u32[]{:S(2)}, u32[]{:S(2)}) %collective-permute-start.2) | collective-permute-done | bytes 1572896 | tf_op jit(solution)/shard_map/ppermute | solution.py:11
  233.4 0.0 copy-done.3
  233.4 1.9 collective-permute-start.3
  235.4 0.0 copy-done.7
  235.5 0.0 copy-done.6
  235.5 0.0 copy-start.4
  235.5 0.1 dynamic_slice.21
  235.6 0.0 copy-done.5
  235.6 0.7 fusion.38
  236.3 3.8 %fusion.28 = (f32[64,512]{1,0:T(8,128)S(1)}, f32[64,512]{1,0:T(8,128)S(1)}, f32[64,512]{1,0:T(8,128)S(1)}, f32[64,512]{1,0:T(8,128)S(1)}, f32[64,512]{1,0:T(8,128)S(1)}) fusion(f32[]{:T(128)} %bitcast.17, f32[]{:T(128)} %bitcast.8, f32[512]{0:T(512)S(1)} %copy-done.6, f32[64]{0:T(128)S(1)} %dynamic_slice.21, f32[]{:T(128)} %bitcast.15, f32[]{:T(128)} %bitcast.13, ...), kind=kLoop, calls=%fused_computation.44 | loop fusion | flops 229376 | bytes 657688 | tf_op jit(solution)/shard_map/sub | solution.py:18
  240.1 1.8 convolution_negate_fusion.4
  241.9 0.0 copy-done.4
  241.9 0.0 copy-start.2
  241.9 1.1 fusion.6
  243.0 0.3 copy-done.2
  243.3 0.4 convolution_negate_fusion.3
  243.7 34.9 %collective-permute-done.3 = bf16[1536,512]{1,0:T(8,128)(2,1)} collective-permute-done((bf16[1536,512]{1,0:T(8,128)(2,1)}, bf16[1536,512]{1,0:T(8,128)(2,1)}, u32[]{:S(2)}, u32[]{:S(2)}) %collective-permute-start.3) | collective-permute-done | bytes 1572896 | tf_op jit(solution)/shard_map/ppermute | solution.py:11
  278.6 1.9 collective-permute-start.4
  280.5 1.1 convolution_add_fusion.3
  281.6 1.8 convolution_negate_fusion.2
  283.4 2.5 convolution_add_fusion.2
  285.9 1.8 convolution_negate_fusion.1
  287.8 2.5 convolution_add_fusion.1
  290.3 21.0 %collective-permute-done.4 = bf16[1536,512]{1,0:T(8,128)(2,1)S(1)} collective-permute-done((bf16[1536,512]{1,0:T(8,128)(2,1)}, bf16[1536,512]{1,0:T(8,128)(2,1)S(1)}, u32[]{:S(2)}, u32[]{:S(2)}) %collective-permute-start.4) | collective-permute-done | bytes 1572896 | tf_op jit(solution)/shard_map/ppermute | solution.py:11
  311.2 0.4 convolution_negate_fusion
  311.6 2.2 fusion.1
  (2 shorter events, 0.0 us)
Async XLA Ops:
  0.0 1.5 copy-start
  56.0 179.5 %copy-start.7 = (f32[8]{0:T(128)S(1)}, f32[8]{0:T(128)}, u32[]{:S(2)}) copy-start(f32[8]{0:T(128)} %param.9) | copy-start | bytes 100
  56.0 179.5 %copy-start.6 = (f32[512]{0:T(512)S(1)}, f32[512]{0:T(512)}, u32[]{:S(2)}) copy-start(f32[512]{0:T(512)} %param.8) | copy-start | bytes 6148
  56.0 179.6 %copy-start.5 = (f32[64]{0:T(128)S(1)}, f32[64]{0:T(128)}, u32[]{:S(2)}) copy-start(f32[64]{0:T(128)} %param.7) | copy-start | bytes 772
  58.6 64.6 %collective-permute-start = (bf16[1536,512]{1,0:T(8,128)(2,1)}, bf16[1536,512]{1,0:T(8,128)(2,1)S(1)}, u32[]{:S(2)}, u32[]{:S(2)}) collective-permute-start(bf16[1536,512]{1,0:T(8,128)(2,1)} %copy.9), channel_id=1, source_target_pairs={{0,16},{8,24},{16,32},{24,40},{32,48},{40,56},{48,64},{56,72},{64,... | collective-permute-start | bytes 4718600 | tf_op jit(solution)/shard_map/ppermute | solution.py:11
  123.2 110.2 %copy-start.3 = (bf16[1536,512]{1,0:T(8,128)(2,1)}, bf16[1536,512]{1,0:T(8,128)(2,1)S(1)}, u32[]{:S(2)}) copy-start(bf16[1536,512]{1,0:T(8,128)(2,1)S(1)} %collective-permute-done) | copy-start | bytes 4718596
  123.2 45.8 %collective-permute-start.1 = (bf16[1536,512]{1,0:T(8,128)(2,1)S(1)}, bf16[1536,512]{1,0:T(8,128)(2,1)S(1)}, u32[]{:S(2)}, u32[]{:S(2)}) collective-permute-start(bf16[1536,512]{1,0:T(8,128)(2,1)S(1)} %collective-permute-done), channel_id=1, source_target_pairs={{0,504},{8,0},{16,8},{24,16},{32,24},{40,32},{48,40},{56,48},{64,5... | collective-permute-start | bytes 4718600 | tf_op jit(solution)/shard_map/ppermute | solution.py:11
  169.1 1.2 copy-start.1
  170.3 63.2 %collective-permute-start.2 = (bf16[1536,512]{1,0:T(8,128)(2,1)S(1)}, bf16[1536,512]{1,0:T(8,128)(2,1)}, u32[]{:S(2)}, u32[]{:S(2)}) collective-permute-start(bf16[1536,512]{1,0:T(8,128)(2,1)S(1)} %collective-permute-done.1), channel_id=1, source_target_pairs={{0,504},{8,0},{16,8},{24,16},{32,24},{40,32},{48,40},{56,48},{64,5... | collective-permute-start | bytes 4718600 | tf_op jit(solution)/shard_map/ppermute | solution.py:11
  233.4 45.2 %collective-permute-start.3 = (bf16[1536,512]{1,0:T(8,128)(2,1)}, bf16[1536,512]{1,0:T(8,128)(2,1)}, u32[]{:S(2)}, u32[]{:S(2)}) collective-permute-start(bf16[1536,512]{1,0:T(8,128)(2,1)} %collective-permute-done.2), channel_id=1, source_target_pairs={{0,504},{8,0},{16,8},{24,16},{32,24},{40,32},{48,40},{56,48},{64,5... | collective-permute-start | bytes 4718600 | tf_op jit(solution)/shard_map/ppermute | solution.py:11
  235.5 6.4 %copy-start.4 = (bf16[1536,512]{1,0:T(8,128)(2,1)S(1)}, bf16[1536,512]{1,0:T(8,128)(2,1)}, u32[]{:S(2)}) copy-start(bf16[1536,512]{1,0:T(8,128)(2,1)} %copy-done.3) | copy-start | bytes 4718596
  241.9 1.4 copy-start.2
  278.6 32.6 %collective-permute-start.4 = (bf16[1536,512]{1,0:T(8,128)(2,1)}, bf16[1536,512]{1,0:T(8,128)(2,1)S(1)}, u32[]{:S(2)}, u32[]{:S(2)}) collective-permute-start(bf16[1536,512]{1,0:T(8,128)(2,1)} %collective-permute-done.3), channel_id=1, source_target_pairs={{0,504},{8,0},{16,8},{24,16},{32,24},{40,32},{48,40},{56,48},{64,5... | collective-permute-start | bytes 4718600 | tf_op jit(solution)/shard_map/ppermute | solution.py:11
